TPU v7x, 256 devices: a whole 4x4x8 slice. The times are simulated.
256 devices in a mesh: section: 32 (over z_lo, y, x), tp: 8 (over z_hi, core).
Axes of the slice: x: 4, y: 4, z: 8 (z_hi: 4, z_lo: 2; z = z_hi * 2 + z_lo), core: 2. Of those that a mesh axis runs over, the one named last changes fastest.
Arguments:
- prefill_hidden: bfloat16 [8192, 8192], P('section', 'tp'), may hold values from -180 to 180
- norm_gain: float32 [8192], replicated, may hold values from 0.25 to 1.75
- key_weight: bfloat16 [8192, 1024], P(None, 'tp'), may hold values from -0.0625 to 0.0625
- value_weight: bfloat16 [8192, 1024], P(None, 'tp'), may hold values from -0.0625 to 0.0625
- prefill_query: bfloat16 [8192, 8192], P('section', 'tp'), may hold values from -102 to 102
- resident_keys: bfloat16 [8192, 16, 1024], P('section', None, 'tp'), may hold values from -6 to 6
- resident_values: bfloat16 [8192, 16, 1024], P('section', None, 'tp'), may hold values from -6 to 6
- decode_query: bfloat16 [512, 8192], P('section', 'tp'), may hold values from -102 to 102
- page_owner: int32 [512], P('section'), may hold values from 0 to 31, as said below
- block_table: int32 [512, 64], P('section'), may hold values from 0 to 319, as said below
- context_len: int32 [512], P('section'), may hold values from 1 to 1024, as said below
Outputs:
- prefill_attention: bfloat16 [8192, 8192], P('section', 'tp')
- decode_attention: bfloat16 [512, 8192], P('section', 'tp')
Inputs may be any that keep to these rules, and one draw needn't show every extreme that they name: `page_owner`: the 16 pages of each section device go to 8 different owners, exactly 2 pages to each; one owner receives pages from every section device. `block_table`: row entries name first the row's resident pages (below 256), then 256 + page_slot for at most 4 pages sent to the row's owner; every page sent to an owner is named by exactly one of its rows; entries after a row's pages are 0. `context_len`: A row's last visible token lies in the last page its table names.
All inputs are finite; a program needn't handle non-finite values.
Results may differ from a plain program's by a relative error of at most 0.011.
Values may be sent and summed in bfloat16 or wider, within the bound.
A program may use at most 192 MiB of HBM per device.

v0:
```python
import math
import jax
import jax.numpy as jnp
from jax import lax
from jax.sharding import PartitionSpec as P

HD = 128
PAGE = 16
CAP = 2
NORM_EPSILON = 1e-05
ROPE_THETA = 500000.0
NEG_LARGE = -1e30


def rotate_keys(raw_keys, positions):
    head_width = raw_keys.shape[-1]
    half_width = head_width // 2
    frequency = jnp.exp(
        jnp.arange(half_width, dtype=jnp.float32) * (-2.0 * math.log(ROPE_THETA) / head_width)
    )
    angles = positions.astype(jnp.float32)[:, None] * frequency[None, :]
    cosine = jnp.cos(angles)[:, None, :]
    sine_part = jnp.sin(angles)[:, None, :]
    first_half = raw_keys[..., :half_width]
    second_half = raw_keys[..., half_width:]
    return jnp.concatenate(
        [
            first_half * cosine - second_half * sine_part,
            second_half * cosine + first_half * sine_part,
        ],
        axis=-1,
    )


def empty_state(kv_heads, group_size, query_rows, head_width):
    return (
        jnp.full((kv_heads, group_size, query_rows), NEG_LARGE, jnp.float32),
        jnp.zeros((kv_heads, group_size, query_rows), jnp.float32),
        jnp.zeros((kv_heads, group_size, query_rows, head_width), jnp.float32),
    )


def attend_piece(carried, queries, query_pos, key_piece, value_piece, key_pos, score_scale):
    kv_heads = queries.shape[1]
    head_width = queries.shape[3]

    def compute(current):
        row_max, row_sum, weighted = current
        piece_rows = key_piece.shape[0]
        key_block = key_piece.reshape(piece_rows, kv_heads, head_width)
        value_block = value_piece.reshape(piece_rows, kv_heads, head_width)
        scores = (
            jnp.einsum("tkgd,rkd->kgtr", queries, key_block, preferred_element_type=jnp.float32)
            * score_scale
        )
        visible = key_pos[None, :] <= query_pos[:, None]
        scores = jnp.where(visible, scores, NEG_LARGE)
        new_max = jnp.maximum(row_max, jnp.max(scores, axis=-1))
        weights = jnp.where(visible, jnp.exp(scores - new_max[..., None]), 0.0)
        new_sum = jnp.sum(weights, axis=-1)
        product = jnp.einsum(
            "kgtr,rkd->kgtd",
            weights.astype(jnp.bfloat16),
            value_block,
            preferred_element_type=jnp.float32,
        )
        return (new_max, new_sum, product)

    return lax.cond(
        jnp.min(key_pos) > jnp.max(query_pos), lambda current: current, compute, carried
    )


def finish_state(carried):
    row_max, row_sum, weighted = carried
    result = weighted / row_sum[..., None]
    kv_heads, group_size, query_rows, head_width = result.shape
    return (
        jnp.transpose(result, (2, 0, 1, 3))
        .reshape(query_rows, kv_heads * group_size * head_width)
        .astype(jnp.bfloat16)
    )


def per_device(
    prefill_hidden,
    norm_gain,
    key_weight,
    value_weight,
    prefill_query,
    resident_keys,
    resident_values,
    decode_query,
    page_owner,
    block_table,
    context_len,
):
    section_count = lax.axis_size("section")
    section_index = lax.axis_index("section")
    stretch_rows = prefill_hidden.shape[0]
    key_width = key_weight.shape[1]
    head_width = HD
    kv_heads = key_width // head_width
    query_width = prefill_query.shape[1]
    group_size = query_width // key_width
    score_scale = 1.0 / math.sqrt(head_width)
    features = lax.all_gather(prefill_hidden, "tp", axis=1, tiled=True)
    feature_f32 = features.astype(jnp.float32)
    inverse_rms = lax.rsqrt(
        jnp.mean(feature_f32 * feature_f32, axis=1, keepdims=True) + NORM_EPSILON
    )
    normed = (feature_f32 * inverse_rms * norm_gain).astype(jnp.bfloat16)
    raw_keys = jnp.dot(normed, key_weight, preferred_element_type=jnp.float32)
    value_rows = jnp.dot(normed, value_weight, preferred_element_type=jnp.float32).astype(
        jnp.bfloat16
    )
    positions = section_index * stretch_rows + jnp.arange(stretch_rows, dtype=jnp.int32)
    key_rows = (
        rotate_keys(raw_keys.reshape(stretch_rows, kv_heads, head_width), positions)
        .reshape(stretch_rows, key_width)
        .astype(jnp.bfloat16)
    )
    queries = prefill_query.reshape(stretch_rows, kv_heads, group_size, head_width)
    pieces = (
        lax.all_gather(key_rows, "section", axis=0, tiled=True),
        lax.all_gather(value_rows, "section", axis=0, tiled=True),
    )
    key_pos = jnp.arange(pieces[0].shape[0], dtype=jnp.int32)
    folded = attend_piece(
        empty_state(kv_heads, group_size, stretch_rows, head_width),
        queries,
        positions,
        pieces[0],
        pieces[1],
        key_pos,
        score_scale,
    )
    prefill_attention = finish_state(folded)
    pages_here = stretch_rows // PAGE
    page_data = jnp.concatenate([key_rows, value_rows], axis=1).reshape(
        pages_here, PAGE * 2 * key_width
    )
    page_index = jnp.arange(pages_here, dtype=jnp.int32)
    same_owner = (page_owner[:, None] == page_owner[None, :]) & (
        page_index[None, :] < page_index[:, None]
    )
    page_rank = jnp.sum(same_owner.astype(jnp.int32), axis=1)
    slot_index = page_owner * CAP + page_rank
    placement_matrix = (
        jnp.arange(section_count * CAP, dtype=jnp.int32)[:, None] == slot_index[None, :]
    ).astype(jnp.bfloat16)
    outgoing = jnp.dot(placement_matrix, page_data, preferred_element_type=jnp.float32).astype(
        jnp.bfloat16
    )
    outgoing = outgoing.reshape(section_count, CAP, PAGE * 2 * key_width)
    arrived = lax.all_to_all(outgoing, "section", split_axis=0, concat_axis=0, tiled=True).reshape(
        section_count * CAP, PAGE, 2 * key_width
    )
    cache_keys = jnp.concatenate([resident_keys, arrived[:, :, :key_width]], axis=0)
    cache_values = jnp.concatenate([resident_values, arrived[:, :, key_width:]], axis=0)
    decode_rows = decode_query.shape[0]
    key_span = block_table.shape[1] * PAGE
    gathered_keys = cache_keys[block_table].reshape(decode_rows, key_span, kv_heads, head_width)
    gathered_values = cache_values[block_table].reshape(decode_rows, key_span, kv_heads, head_width)
    decode_queries = decode_query.reshape(decode_rows, kv_heads, group_size, head_width)
    scores = (
        jnp.einsum(
            "bkgd,blkd->bkgl", decode_queries, gathered_keys, preferred_element_type=jnp.float32
        )
        * score_scale
    )
    visible = (jnp.arange(key_span, dtype=jnp.int32)[None, :] < context_len[:, None])[
        :, None, None, :
    ]
    scores = jnp.where(visible, scores, NEG_LARGE)
    row_max = jnp.max(scores, axis=-1, keepdims=True)
    weights = jnp.exp(scores - row_max)
    row_sum = jnp.sum(weights, axis=-1, keepdims=True)
    attended = (
        jnp.einsum(
            "bkgl,blkd->bkgd",
            weights.astype(jnp.bfloat16),
            gathered_values,
            preferred_element_type=jnp.float32,
        )
        / row_sum
    )
    decode_attention = attended.reshape(decode_rows, query_width).astype(jnp.bfloat16)
    return (prefill_attention, decode_attention)


def solution(mesh):
    return jax.shard_map(
        per_device,
        mesh=mesh,
        in_specs=(
            P("section", "tp"),
            P(),
            P(None, "tp"),
            P(None, "tp"),
            P("section", "tp"),
            P("section", None, "tp"),
            P("section", None, "tp"),
            P("section", "tp"),
            P("section"),
            P("section", None),
            P("section"),
        ),
        out_specs=(P("section", "tp"), P("section", "tp")),
        check_vma=False,
    )
```

profile of v0, /device:TPU:24, one launch (start us, length us, event | category | flops | bytes accessed | tf_op | source)
XLA Modules:
  0.0 413.2 jit_solution(1083435418822819909)
XLA Ops:
  7.2 0.0 copy-start
  7.2 0.0 all-gather.5.cloned.1.call-start
  7.2 0.7 all-gather.5.cloned.1.call-update
  7.9 0.0 all-gather.9.cloned.1.call-start
  8.0 56.6 %all-gather.5.cloned.1.call-done = bf16[256,8192]{1,0:T(8,128)(2,1)} async-done(((bf16[256,1024]{1,0:T(8,128)(2,1)}), bf16[256,8192]{1,0:T(8,128)(2,1)}) %all-gather.5.cloned.1.call-update) | async-done | bytes 4194320 | tf_op jit(solution)/shard_map/all_gather | solution.py:107
  64.6 3.3 fusion.20
  67.9 0.2 copy-done.2
  68.1 1.7 fusion.29
  69.8 0.3 fusion.46
  70.1 0.6 fusion.53
  70.8 0.0 all-gather.9.cloned.1.call-update
  70.8 0.0 copy-start.8
  70.8 0.0 copy-start.4
  70.8 0.0 copy-start.3
  70.8 0.0 copy-start.5
  70.8 0.0 all-gather.7.cloned.1.call-start
  70.9 5.2 %fusion.32 = bf16[256,128]{0,1:T(8,128)(2,1)} fusion(bf16[8192,128]{1,0:T(8,128)(2,1)} %param.16, bf16[256,8192]{1,0:T(8,128)(2,1)} %all-gather.5.cloned.1.call-done, f32[8192]{0:T(1024)S(1)} %copy-done.7, f32[256]{0:T(256)S(1)} %add_rsqrt_fusion), kind=kOutput, calls=%fused_computation.35 | convolution fusion | flops 545292288 | bytes 6390784 | tf_op jit(solution)/shard_map/dot_general | solution.py:114
  76.1 0.0 all-gather.7.cloned.1.call-update
  76.2 0.2 convert_reduce_fusion
  76.4 0.9 pad_maximum_fusion.2
  77.2 0.1 copy.30
  77.3 0.1 reshape.215
  77.4 0.3 convolution_convert_fusion
  77.7 1.1 reshape.216
  78.8 8.9 %all-to-all-start = ((bf16[32,2,4096]{2,1,0:T(2,128)(2,1)}), bf16[32,2,4096]{2,1,0:T(2,128)(2,1)S(1)}, u32[]{:S(2)}, u32[]{:S(2)}) async-start(bf16[32,2,4096]{2,1,0:T(2,128)(2,1)} %reshape.216), calls=%async_computation | async-start | bytes 1048576 | tf_op jit(solution)/shard_map/all_to_all | solution.py:156
  87.7 0.6 fusion.52
  88.4 0.1 reshape.223
  89.1 0.1 iota_compare_fusion
  89.2 9.3 %all-to-all-done = bf16[32,2,4096]{2,1,0:T(2,128)(2,1)S(1)} async-done(((bf16[32,2,4096]{2,1,0:T(2,128)(2,1)}), bf16[32,2,4096]{2,1,0:T(2,128)(2,1)S(1)}, u32[]{:S(2)}, u32[]{:S(2)}) %all-to-all-start) | async-done | bytes 524320 | tf_op jit(solution)/shard_map/all_to_all | solution.py:156
  98.5 0.3 reshape.217
  98.8 0.1 fusion.54
  98.9 2.8 pad_maximum_fusion
  101.8 9.6 %gather_fusion = bf16[1024,16,128]{2,1,0:T(8,128)(2,1)} fusion(bf16[320,16,128]{2,1,0:T(8,128)(2,1)} %get-tuple-element.49, s32[1024]{0:T(1024)S(1)} %broadcast_clamp_fusion), kind=kCustom, calls=%fused_computation | custom fusion | bytes 8392704 | tf_op jit(solution)/shard_map/gather | solution.py:163
  111.4 8.4 %gather_fusion.1 = bf16[1024,16,128]{2,1,0:T(8,128)(2,1)} fusion(bf16[320,16,128]{2,1,0:T(8,128)(2,1)S(1)} %get-tuple-element.50, s32[1024]{0:T(1024)S(1)} %broadcast_clamp_fusion), kind=kCustom, calls=%fused_computation.1 | custom fusion | bytes 8392704 | tf_op jit(solution)/shard_map/gather | solution.py:164
  119.7 3.6 fusion.55
  123.3 0.2 fusion.37
  123.6 0.7 fusion.35
  124.3 0.6 copy.49
  124.9 72.8 %all-gather.9.cloned.1.call-done = bf16[8192,1,128]{0,2,1:T(8,128)(2,1)} async-done(((bf16[256,1,128]{0,2,1:T(8,128)(2,1)}), bf16[8192,1,128]{0,2,1:T(8,128)(2,1)}) %all-gather.9.cloned.1.call-update) | async-done | bytes 2097168 | tf_op jit(solution)/shard_map/all_gather | solution.py:125
  197.7 127.6 %all-gather.7.cloned.1.call-done = bf16[8192,128]{0,1:T(8,128)(2,1)} async-done(((bf16[256,128]{0,1:T(8,128)(2,1)}), bf16[8192,128]{0,1:T(8,128)(2,1)}) %all-gather.7.cloned.1.call-update) | async-done | bytes 2097168 | tf_op jit(solution)/shard_map/all_gather | solution.py:126
  325.3 79.7 %conditional.1 = (f32[1,8,256]{2,1,0:T(8,128)S(1)}, f32[1,8,256,128]{3,2,1,0:T(8,128)S(1)}) conditional(s32[]{:T(128)} %convert_element_type.52, (s32[8192]{0:T(1024)S(1)}, s32[256]{0:T(256)S(1)}, bf16[256,1024]{1,0:T(8,128)(2,1)S(1)}, bf16[8192,128]{0,1:T(8,128)(2,1)}, bf16[8192,128]{0,1:T(8,128)(2,1)}) %tuple.37, () %tuple.17), branch_computations={%region_2.5_spmd, %region_5.0_spmd} | conditional | flops 8810133504 | bytes 215565328 | solution.py:69
  325.4 4.7 %broadcast_compare_fusion = pred[256,8192]{0,1:T(8,128)(4,1)} fusion(s32[256]{0:T(256)S(1)} %get-tuple-element.12, s32[8192]{0:T(1024)S(1)} %get-tuple-element.11), kind=kLoop, calls=%fused_computation.10 | loop fusion | flops 2097152 | bytes 2130944 | tf_op jit(solution)/shard_map/cond/branch_0_fun/le | solution.py:56
  330.0 25.5 %fusion = (f32[8,256]{1,0:T(8,128)S(1)}, f32[8192,256,8]{1,0,2:T(8,128)}) fusion(pred[256,8192]{0,1:T(8,128)(4,1)} %broadcast_compare_fusion, bf16[8192,128]{0,1:T(8,128)(2,1)} %get-tuple-element.37, bf16[256,1024]{1,0:T(8,128)(2,1)S(1)} %get-tuple-element.23), kind=kOutput, calls=%fused_computation.4 | convolution fusion | flops 4345296896 | bytes 71835648 | tf_op jit(solution)/shard_map/cond/branch_0_fun/tkgd,rkd->kgtr/dot_general | solution.py:53
  355.6 27.2 %fusion.10 = f32[1,8,256,128]{3,2,1,0:T(8,128)S(1)} fusion(bf16[8192,128]{0,1:T(8,128)(2,1)} %get-tuple-element.38, f32[8192,256,8]{1,0,2:T(8,128)} %get-tuple-element.40, f32[8,256]{1,0:T(8,128)S(1)} %broadcast_maximum_fusion, pred[256,8192]{0,1:T(8,128)(4,1)} %broadcast_compare_fusion), kind=kOutput, calls=%fused_computation.14 | convolution fusion | flops 4378853376 | bytes 72359936 | tf_op jit(solution)/shard_map/cond/branch_0_fun/kgtr,rkd->kgtd/dot_general | solution.py:61
  382.8 22.3 %fusion.2 = f32[8,256]{1,0:T(8,128)S(1)} fusion(f32[8192,256,8]{1,0,2:T(8,128)} %get-tuple-element.40, f32[8,256]{1,0:T(8,128)S(1)} %broadcast_maximum_fusion, pred[256,8192]{0,1:T(8,128)(4,1)} %broadcast_compare_fusion), kind=kLoop, calls=%fused_computation.6 | loop fusion | flops 83884032 | bytes 69222400 | tf_op jit(solution)/shard_map/cond/branch_0_fun/reduce_sum | solution.py:60
  405.0 0.3 fusion.36
  405.4 0.3 copy.29
  405.7 0.9 copy.48
  (22 shorter events, 0.1 us)
Async XLA Ops:
  7.2 60.7 %copy-start = (bf16[8192,128]{1,0:T(8,128)(2,1)S(1)}, bf16[8192,128]{1,0:T(8,128)(2,1)}, u32[]{:S(2)}) copy-start(bf16[8192,128]{1,0:T(8,128)(2,1)} %param.15) | copy-start | bytes 6291460
  7.2 60.7 %copy-start.7 = (f32[8192]{0:T(1024)S(1)}, f32[8192]{0:T(1024)}, u32[]{:S(2)}) copy-start(f32[8192]{0:T(1024)} %param.14) | copy-start | bytes 98308
  7.2 57.4 %all-gather.5.cloned.1.call-start = ((), (), s32[]{:S(2)}) async-start(), calls=%async_computation.1 | async-start | bytes 4718592 | tf_op jit(solution)/shard_map/all_gather | solution.py:107
  7.9 189.8 %all-gather.9.cloned.1.call-start = ((), (), s32[]{:S(2)}) async-start(), calls=%async_computation.3 | async-start | bytes 2162688 | tf_op jit(solution)/shard_map/all_gather | solution.py:125
  64.6 3.4 copy-start.2
  70.8 5.4 %copy-start.8 = (s32[16]{0:T(128)S(1)}, s32[16]{0:T(128)}, u32[]{:S(2)}) copy-start(s32[16]{0:T(128)} %param.21) | copy-start | bytes 196
  70.8 17.6 %copy-start.4 = (s32[16,64]{1,0:T(8,128)S(1)}, s32[16,64]{1,0:T(8,128)}, u32[]{:S(2)}) copy-start(s32[16,64]{1,0:T(8,128)} %param.22) | copy-start | bytes 12292
  70.8 17.6 %copy-start.3 = (bf16[16,1024]{1,0:T(8,128)(2,1)S(1)}, bf16[16,1024]{1,0:T(8,128)(2,1)}, u32[]{:S(2)}) copy-start(bf16[16,1024]{1,0:T(8,128)(2,1)} %param.20) | copy-start | bytes 98308
  70.8 18.3 %copy-start.5 = (s32[16]{0:T(128)S(1)}, s32[16]{0:T(128)}, u32[]{:S(2)}) copy-start(s32[16]{0:T(128)} %param.23) | copy-start | bytes 196
  70.8 254.5 %all-gather.7.cloned.1.call-start = ((), (), s32[]{:S(2)}) async-start(), calls=%async_computation.2 | async-start | bytes 2162688 | tf_op jit(solution)/shard_map/all_gather | solution.py:126
  78.8 19.7 %all-to-all-start = ((bf16[32,2,4096]{2,1,0:T(2,128)(2,1)}), bf16[32,2,4096]{2,1,0:T(2,128)(2,1)S(1)}, u32[]{:S(2)}, u32[]{:S(2)}) async-start(bf16[32,2,4096]{2,1,0:T(2,128)(2,1)} %reshape.216), calls=%async_computation | async-start | bytes 1048576 | tf_op jit(solution)/shard_map/all_to_all | solution.py:156
  119.7 3.8 copy-start.1
  119.7 205.6 %copy-start.6 = (bf16[256,1024]{1,0:T(8,128)(2,1)S(1)}, bf16[256,1024]{1,0:T(8,128)(2,1)}, u32[]{:S(2)}) copy-start(bf16[256,1024]{1,0:T(8,128)(2,1)} %param.17) | copy-start | bytes 1572868
Sparse Core Ops, SparseCore 0:
  9.8 54.7 all-gather.4
  70.9 126.7 all-gather.8
  199.4 125.8 all-gather.6
where the time goes:
time: 413 us
  waiting for transfers between devices  267 us (65%)
  matrix products  64.3 us (16%)
  other arithmetic  36.3 us (9%)
  local copies, waits for them, and re-layouts  21.9 us (5%)
  between operations  14.6 us (4%)
  starting transfers between devices  9.03 us (2%)
    all_gather x1, waiting for transfers between devices, per_device(): lax.all_gather(value_rows, 'section', axis=0, tiled=True)  128 us
    all_gather x1, waiting for transfers between devices, per_device(): lax.all_gather(key_rows, 'section', axis=0, tiled=True)  72.8 us
    all_gather x1, waiting for transfers between devices, per_device(): features = lax.all_gather(prefill_hidden, 'tp', axis=1, tiled=True)  56.6 us
    dot_general x1, matrix products, compute(): jnp.einsum('kgtr,rkd->kgtd', weights.astype(jnp.bfloat16), value_block, p...  27.2 us
    dot_general x1, matrix products, compute(): jnp.einsum('tkgd,rkd->kgtr', queries, key_block, preferred_element_type=j...  25.5 us
    reduce_sum x1, other arithmetic, compute(): new_sum = jnp.sum(weights, axis=-1)  22.3 us
    gather x1, local copies, waits for them, and re-layouts, per_device(): cache_keys[block_table].reshape(decode_rows, key_span, kv_heads, head_width)  9.61 us
    all_to_all x1, waiting for transfers between devices, per_device(): lax.all_to_all(outgoing, 'section', split_axis=0, concat_axis=0, tiled=True)  9.27 us
  transfers between devices with their start and end apart: 4, of which 4 were waited for; matrix products, arithmetic and copies ran while one was open for 8% of the time, Pallas kernels for 0%

commit v1 on v0

--- a/solution.py
+++ b/solution.py
@@ -10,6 +10,13 @@
 NORM_EPSILON = 1e-05
 ROPE_THETA = 500000.0
 NEG_LARGE = -1e30
+
+
+def exchange_gather(block, axis, along):
+    size = lax.axis_size(axis)
+    shards = jnp.stack([block for _ in range(size)])
+    shards = lax.all_to_all(shards, axis, split_axis=0, concat_axis=0)
+    return jnp.concatenate(shards, axis=along)
 
 
 def rotate_keys(raw_keys, positions):
@@ -123,7 +130,7 @@
     queries = prefill_query.reshape(stretch_rows, kv_heads, group_size, head_width)
     pieces = (
         lax.all_gather(key_rows, "section", axis=0, tiled=True),
-        lax.all_gather(value_rows, "section", axis=0, tiled=True),
+        exchange_gather(value_rows, "section", 0),
     )
     key_pos = jnp.arange(pieces[0].shape[0], dtype=jnp.int32)
     folded = attend_piece(

time: 413 us -> 310 us (0.75)
  waiting for transfers between devices: 267 us -> 157 us
  starting transfers between devices: 9.03 us -> 14.9 us
    all_gather x1 -> x0, waiting for transfers between devices: 128 us -> none  [per_device(): lax.all_gather(value_rows, 'section', axis=0, tiled=True)]
    all_gather x1, waiting for transfers between devices: 72.8 us -> 91 us  [per_device(): lax.all_gather(key_rows, 'section', axis=0, tiled=True)]
    all_to_all x0 -> x1, starting transfers between devices: none -> 5.87 us  [exchange_gather(): shards = lax.all_to_all(shards, axis, split_axis=0, concat_axis=0)]
  transfers between devices with their start and end apart: 4 -> 4, of which waited for: 4 -> 3; matrix products, arithmetic and copies ran while one was open for 8% -> 10% of each run, Pallas kernels for 0% -> 0%
where the time goes in v1:
time: 310 us; the launch traced here: 309 us
  waiting for transfers between devices  157 us (51%)
  matrix products  60.6 us (20%)
  other arithmetic  36.9 us (12%)
  local copies, waits for them, and re-layouts  23.9 us (8%)
  starting transfers between devices  14.9 us (5%)
  between operations  14.9 us (5%)
    all_gather x1, waiting for transfers between devices, per_device(): lax.all_gather(key_rows, 'section', axis=0, tiled=True)  91 us
    all_gather x1, waiting for transfers between devices, per_device(): features = lax.all_gather(prefill_hidden, 'tp', axis=1, tiled=True)  55.1 us
    dot_general x1, matrix products, compute(): jnp.einsum('kgtr,rkd->kgtd', weights.astype(jnp.bfloat16), value_block, p...  27.1 us
    dot_general x1, matrix products, compute(): jnp.einsum('tkgd,rkd->kgtr', queries, key_block, preferred_element_type=j...  25.5 us
    reduce_sum x1, other arithmetic, compute(): new_sum = jnp.sum(weights, axis=-1)  22.3 us
    all_to_all x1, waiting for transfers between devices, per_device(): lax.all_to_all(outgoing, 'section', split_axis=0, concat_axis=0, tiled=True)  9.98 us
    gather x1, local copies, waits for them, and re-layouts, per_device(): cache_keys[block_table].reshape(decode_rows, key_span, kv_heads, head_width)  9.64 us
    all_to_all x1, starting transfers between devices, per_device(): lax.all_to_all(outgoing, 'section', split_axis=0, concat_axis=0, tiled=True)  8.91 us
  transfers between devices with their start and end apart: 4, of which 3 were waited for; matrix products, arithmetic and copies ran while one was open for 10% of the time, Pallas kernels for 0%

profile of v1, /device:TPU:24, one launch (start us, length us, event | category | flops | bytes accessed | tf_op | source)
XLA Modules:
  0.0 308.8 jit_solution(10768335590187252116)
XLA Ops:
  7.2 0.0 copy-start
  7.2 0.0 all-gather.4.cloned.1.call-start
  7.2 0.7 all-gather.4.cloned.1.call-update
  8.0 0.9 convert_reduce_fusion
  8.9 0.7 multiply_add_fusion
  9.5 55.1 %all-gather.4.cloned.1.call-done = bf16[256,8192]{1,0:T(8,128)(2,1)} async-done(((bf16[256,1024]{1,0:T(8,128)(2,1)}), bf16[256,8192]{1,0:T(8,128)(2,1)}) %all-gather.4.cloned.1.call-update) | async-done | bytes 4194320 | tf_op jit(solution)/shard_map/all_gather | solution.py:114
  64.6 3.3 %fusion.17 = f32[256]{0:T(256)S(1)} fusion(bf16[256,8192]{1,0:T(8,128)(2,1)} %all-gather.4.cloned.1.call-done), kind=kLoop, calls=%fused_computation.22 | loop fusion | flops 6291200 | bytes 4195328 | tf_op jit(solution)/shard_map/reduce_sum | solution.py:117
  67.9 0.2 copy-done.2
  68.1 1.7 fusion.26
  69.8 0.3 fusion.43
  70.1 0.6 fusion.50
  70.8 1.7 fusion.29
  72.5 0.1 copy.30
  72.7 0.1 reshape.218
  72.7 0.3 convolution_convert_fusion
  73.0 0.0 copy-start.4
  73.0 0.0 copy-start.3
  73.0 0.0 copy-start.5
  73.0 1.1 reshape.219
  74.2 8.9 %all-to-all-start.1 = ((bf16[32,2,4096]{2,1,0:T(2,128)(2,1)}), bf16[32,2,4096]{2,1,0:T(2,128)(2,1)S(1)}, u32[]{:S(2)}, u32[]{:S(2)}) async-start(bf16[32,2,4096]{2,1,0:T(2,128)(2,1)} %reshape.219), calls=%async_computation.1 | async-start | bytes 1048576 | tf_op jit(solution)/shard_map/all_to_all | solution.py:163
  83.1 0.0 all-gather.6.cloned.1.call-start
  83.1 0.1 copy.27
  83.3 0.6 all-gather.6.cloned.1.call-update
  83.8 10.0 %all-to-all-done.1 = bf16[32,2,4096]{2,1,0:T(2,128)(2,1)S(1)} async-done(((bf16[32,2,4096]{2,1,0:T(2,128)(2,1)}), bf16[32,2,4096]{2,1,0:T(2,128)(2,1)S(1)}, u32[]{:S(2)}, u32[]{:S(2)}) %all-to-all-start.1) | async-done | bytes 524320 | tf_op jit(solution)/shard_map/all_to_all | solution.py:163
  93.8 1.8 stack.2
  95.7 5.9 %all-to-all-start = ((bf16[32,256,128]{2,1,0:T(8,128)(2,1)}), bf16[32,256,128]{2,1,0:T(8,128)(2,1)}, u32[]{:S(2)}, u32[]{:S(2)}) async-start(bf16[32,256,128]{2,1,0:T(8,128)(2,1)} %stack.2), calls=%async_computation | async-start | bytes 4194304 | tf_op jit(solution)/shard_map/all_to_all | solution.py:18
  101.5 0.6 fusion.49
  102.2 0.1 reshape.226
  103.0 0.1 iota_compare_fusion
  103.0 0.3 reshape.220
  103.4 0.1 fusion.51
  103.5 2.8 pad_maximum_fusion
  106.3 9.6 %gather_fusion = bf16[1024,16,128]{2,1,0:T(8,128)(2,1)} fusion(bf16[320,16,128]{2,1,0:T(8,128)(2,1)} %get-tuple-element.49, s32[1024]{0:T(1024)S(1)} %broadcast_clamp_fusion), kind=kCustom, calls=%fused_computation | custom fusion | bytes 8392704 | tf_op jit(solution)/shard_map/gather | solution.py:170
  116.0 8.4 %gather_fusion.1 = bf16[1024,16,128]{2,1,0:T(8,128)(2,1)} fusion(bf16[320,16,128]{2,1,0:T(8,128)(2,1)S(1)} %get-tuple-element.50, s32[1024]{0:T(1024)S(1)} %broadcast_clamp_fusion), kind=kCustom, calls=%fused_computation.1 | custom fusion | bytes 8392704 | tf_op jit(solution)/shard_map/gather | solution.py:171
  124.3 3.6 %fusion.52 = (f32[16,8]{1,0:T(8,128)S(1)}, f32[16,8,1024]{2,1,0:T(8,128)S(1)}) fusion(bf16[16,1024,128]{2,1,0:T(8,128)(2,1)} %bitcast.74, bf16[16,8,128]{2,1,0:T(8,128)(2,1)S(1)} %bitcast.77, pred[16,1024]{1,0:T(8,128)(4,1)S(1)} %iota_compare_fusion), kind=kOutput, calls=%fused_computation.73 | convolution fusion | flops 33947520 | bytes 4768256 | tf_op jit(solution)/shard_map/bkgd,blkd->bkgl/dot_general | solution.py:174
  127.9 0.2 fusion.34
  128.2 0.7 fusion.32
  128.9 0.6 copy.47
  129.5 91.0 %all-gather.6.cloned.1.call-done = bf16[8192,1,128]{0,2,1:T(8,128)(2,1)} async-done(((bf16[256,1,128]{0,2,1:T(8,128)(2,1)}), bf16[8192,1,128]{0,2,1:T(8,128)(2,1)}) %all-gather.6.cloned.1.call-update) | async-done | bytes 2097168 | tf_op jit(solution)/shard_map/all_gather | solution.py:132
  220.5 0.0 all-to-all-done
  220.6 79.8 %conditional.1 = (f32[1,8,256]{2,1,0:T(8,128)S(1)}, f32[1,8,256,128]{3,2,1,0:T(8,128)S(1)}) conditional(s32[]{:T(128)} %convert_element_type.52, (s32[8192]{0:T(1024)S(1)}, s32[256]{0:T(256)S(1)}, bf16[256,1024]{1,0:T(8,128)(2,1)S(1)}, bf16[8192,128]{0,1:T(8,128)(2,1)}, bf16[32,256,128]{2,1,0:T(8,128)(2,1)}) %tuple.35, () %tuple.17), branch_computations={%region_2.5_spmd, %region_5.0_spmd} | conditional | flops 8810133504 | bytes 215565328 | solution.py:76
  220.8 4.7 %broadcast_compare_fusion = pred[256,8192]{0,1:T(8,128)(4,1)} fusion(s32[256]{0:T(256)S(1)} %get-tuple-element.12, s32[8192]{0:T(1024)S(1)} %get-tuple-element.11), kind=kLoop, calls=%fused_computation.10 | loop fusion | flops 2097152 | bytes 2130944 | tf_op jit(solution)/shard_map/cond/branch_0_fun/le | solution.py:63
  225.5 25.5 %fusion = (f32[8,256]{1,0:T(8,128)S(1)}, f32[8192,256,8]{1,0,2:T(8,128)}) fusion(pred[256,8192]{0,1:T(8,128)(4,1)} %broadcast_compare_fusion, bf16[8192,128]{0,1:T(8,128)(2,1)} %get-tuple-element.37, bf16[256,1024]{1,0:T(8,128)(2,1)S(1)} %get-tuple-element.23), kind=kOutput, calls=%fused_computation.4 | convolution fusion | flops 4345296896 | bytes 71835648 | tf_op jit(solution)/shard_map/cond/branch_0_fun/tkgd,rkd->kgtr/dot_general | solution.py:60
  251.0 27.1 %fusion.9 = f32[1,8,256,128]{3,2,1,0:T(8,128)S(1)} fusion(bf16[8192,128,1]{1,0,2:T(8,128)(2,1)} %bitcast.6, f32[8192,256,8]{1,0,2:T(8,128)} %get-tuple-element.40, f32[8,256]{1,0:T(8,128)S(1)} %broadcast_maximum_fusion, pred[256,8192]{0,1:T(8,128)(4,1)} %broadcast_compare_fusion), kind=kOutput, calls=%fused_computation.13 | convolution fusion | flops 4378853376 | bytes 72359936 | tf_op jit(solution)/shard_map/cond/branch_0_fun/kgtr,rkd->kgtd/dot_general | solution.py:68
  278.1 22.3 %fusion.2 = f32[8,256]{1,0:T(8,128)S(1)} fusion(f32[8192,256,8]{1,0,2:T(8,128)} %get-tuple-element.40, f32[8,256]{1,0:T(8,128)S(1)} %broadcast_maximum_fusion, pred[256,8192]{0,1:T(8,128)(4,1)} %broadcast_compare_fusion), kind=kLoop, calls=%fused_computation.6 | loop fusion | flops 83884032 | bytes 69222400 | tf_op jit(solution)/shard_map/cond/branch_0_fun/reduce_sum | solution.py:67
  300.3 0.3 fusion.33
  300.7 0.3 copy.29
  301.0 0.9 copy.46
  (23 shorter events, 0.1 us)
Async XLA Ops:
  7.2 60.7 %copy-start = (bf16[8192,128]{1,0:T(8,128)(2,1)S(1)}, bf16[8192,128]{1,0:T(8,128)(2,1)}, u32[]{:S(2)}) copy-start(bf16[8192,128]{1,0:T(8,128)(2,1)} %param.15) | copy-start | bytes 6291460
  7.2 60.7 %copy-start.8 = (f32[8192]{0:T(1024)S(1)}, f32[8192]{0:T(1024)}, u32[]{:S(2)}) copy-start(f32[8192]{0:T(1024)} %param.14) | copy-start | bytes 98308
  7.2 57.4 %all-gather.4.cloned.1.call-start = ((), (), s32[]{:S(2)}) async-start(), calls=%async_computation.2 | async-start | bytes 4718592 | tf_op jit(solution)/shard_map/all_gather | solution.py:114
  64.6 3.4 %copy-start.2 = (bf16[256,8192]{1,0:T(8,128)(2,1)S(1)}, bf16[256,8192]{1,0:T(8,128)(2,1)}, u32[]{:S(2)}) copy-start(bf16[256,8192]{1,0:T(8,128)(2,1)} %all-gather.4.cloned.1.call-done) | copy-start | bytes 12582916
  68.1 2.7 copy-start.6
  73.0 29.2 %copy-start.4 = (s32[16,64]{1,0:T(8,128)S(1)}, s32[16,64]{1,0:T(8,128)}, u32[]{:S(2)}) copy-start(s32[16,64]{1,0:T(8,128)} %param.22) | copy-start | bytes 12292
  73.0 29.2 %copy-start.3 = (bf16[16,1024]{1,0:T(8,128)(2,1)S(1)}, bf16[16,1024]{1,0:T(8,128)(2,1)}, u32[]{:S(2)}) copy-start(bf16[16,1024]{1,0:T(8,128)(2,1)} %param.20) | copy-start | bytes 98308
  73.0 29.9 %copy-start.5 = (s32[16]{0:T(128)S(1)}, s32[16]{0:T(128)}, u32[]{:S(2)}) copy-start(s32[16]{0:T(128)} %param.23) | copy-start | bytes 196
  74.2 19.7 %all-to-all-start.1 = ((bf16[32,2,4096]{2,1,0:T(2,128)(2,1)}), bf16[32,2,4096]{2,1,0:T(2,128)(2,1)S(1)}, u32[]{:S(2)}, u32[]{:S(2)}) async-start(bf16[32,2,4096]{2,1,0:T(2,128)(2,1)} %reshape.219), calls=%async_computation.1 | async-start | bytes 1048576 | tf_op jit(solution)/shard_map/all_to_all | solution.py:163
  83.1 137.5 %all-gather.6.cloned.1.call-start = ((), (), s32[]{:S(2)}) async-start(), calls=%async_computation.3 | async-start | bytes 2162688 | tf_op jit(solution)/shard_map/all_gather | solution.py:132
  95.7 124.9 %all-to-all-start = ((bf16[32,256,128]{2,1,0:T(8,128)(2,1)}), bf16[32,256,128]{2,1,0:T(8,128)(2,1)}, u32[]{:S(2)}, u32[]{:S(2)}) async-start(bf16[32,256,128]{2,1,0:T(8,128)(2,1)} %stack.2), calls=%async_computation | async-start | bytes 4194304 | tf_op jit(solution)/shard_map/all_to_all | solution.py:18
  124.3 3.8 %copy-start.1 = (bf16[1024,16,128]{2,1,0:T(8,128)(2,1)S(1)}, bf16[1024,16,128]{2,1,0:T(8,128)(2,1)}, u32[]{:S(2)}) copy-start(bf16[1024,16,128]{2,1,0:T(8,128)(2,1)} %gather_fusion.1) | copy-start | bytes 12582916
  124.3 96.2 %copy-start.7 = (bf16[256,1024]{1,0:T(8,128)(2,1)S(1)}, bf16[256,1024]{1,0:T(8,128)(2,1)}, u32[]{:S(2)}) copy-start(bf16[256,1024]{1,0:T(8,128)(2,1)} %param.17) | copy-start | bytes 1572868
Sparse Core Ops, SparseCore 0:
  9.8 54.7 all-gather.3
  85.6 134.8 all-gather.5
